TPU v7x, 128 devices: a whole 4x4x4 slice. The times are simulated.
128 devices in a mesh: req: 16 (over z, y), kv: 8 (over x, core).
Axes of the slice: x: 4, y: 4, z: 4, core: 2. Of those that a mesh axis runs over, the one named last changes fastest.
Arguments:
- hidden_in: bfloat16 [16384, 2048], P(('req', 'kv')), may hold values from -6 to 6
- slot_tokens: int32 [16384], replicated, may hold values from 0 to 16383, as said below
- cache_len: int32 [128], P('req'), may hold values from 1 to 2048, 65536 in all
- prefill_start: int32 [16], P('req'), may hold values from 0 to 2048
- key_cache: bfloat16 [128, 2048, 1024], P('req', None, 'kv')
- value_cache: bfloat16 [128, 2048, 1024], P('req', None, 'kv'), may hold values from -18 to 18
- key_prefix: bfloat16 [16, 2048, 1024], P('req', None, 'kv')
- value_prefix: bfloat16 [16, 2048, 1024], P('req', None, 'kv'), may hold values from -18 to 18
- attn_gain: float32 [2048], replicated, may hold values from 0.25 to 1.75
- q_proj: bfloat16 [2048, 2048], P(None, 'kv'), may hold values from -0.125 to 0.125
- k_proj: bfloat16 [2048, 1024], P(None, 'kv'), may hold values from -0.125 to 0.125
- v_proj: bfloat16 [2048, 1024], P(None, 'kv'), may hold values from -0.125 to 0.125
- q_gain: float32 [128], replicated, may hold values from 0.25 to 1.75
- k_gain: float32 [128], replicated, may hold values from 0.25 to 1.75
- o_proj: bfloat16 [2048, 2048], P('kv'), may hold values from -0.125 to 0.125
- ffn_gain: float32 [2048], replicated, may hold values from 0.25 to 1.75
- w_gate: bfloat16 [2048, 6144], P(None, 'req'), may hold values from -0.125 to 0.125
- w_up: bfloat16 [2048, 6144], P(None, 'req'), may hold values from -0.125 to 0.125
- w_down: bfloat16 [6144, 2048], P('req'), may hold values from -0.078125 to 0.078125
- final_gain: float32 [2048], replicated, may hold values from 0.25 to 1.75
- lm_head: bfloat16 [2048, 151936], P(None, ('req', 'kv')), may hold values from -0.375 to 0.375
Outputs:
- layer_out: bfloat16 [16384, 2048], P(('req', 'kv'))
- max_logit: float32 [144], replicated
Inputs may be any that keep to these rules, and one draw needn't show every extreme that they name: slot_tokens is a permutation of the batch's tokens; each device's 128 consecutive slots take exactly 1 token from each device's 128 consecutive batch tokens.
All inputs are finite; a program needn't handle non-finite values. No bound on the sum of `cache_len` on one device may be relied on, other than what follows from the above.
Results may differ from a plain program's by a relative error of at most 0.0085.
The roundings to bfloat16 on the way count: a program that leaves them out, or rounds other values in their place, can miss the bound.
Values may be sent and summed in bfloat16 or wider, within the bound.
A program may use at most 128 MiB of HBM per device.

v0:
```python
import jax
import jax.numpy as jnp
from jax import lax
from jax.sharding import PartitionSpec as P

EPS = 1e-06
NEG = -1e30


def spread(value, axis, root):
    mine = lax.axis_index(axis) == root
    return lax.psum(jnp.where(mine, value, jnp.zeros_like(value)), axis)


def norm_rows(values, gain_vec):
    wide = values.astype(jnp.float32)
    return wide * lax.rsqrt(jnp.mean(wide * wide, axis=-1, keepdims=True) + EPS) * gain_vec


def rotate(values, places):
    half_dim = values.shape[-1] // 2
    freqs = 1000000.0 ** (-(jnp.arange(half_dim, dtype=jnp.float32) * 2.0 / values.shape[-1]))
    angles = places[:, None] * freqs[None, :]
    cosine = jnp.cos(angles)[:, None, :]
    sine = jnp.sin(angles)[:, None, :]
    first_half = values[..., :half_dim]
    second_half = values[..., half_dim:]
    return jnp.concatenate(
        [first_half * cosine - second_half * sine, second_half * cosine + first_half * sine],
        axis=-1,
    )


def prefill_full(q_heads, key_old, value_old, key_new, value_new, start_at):
    old_len = key_old.shape[0]
    fresh_rows = q_heads.shape[0]
    factor = q_heads.shape[-1] ** (-0.5)
    all_keys = jnp.concatenate([key_old, key_new], axis=0)
    all_values = jnp.concatenate([value_old, value_new], axis=0)
    scores = (
        jnp.einsum("cgd,kd->gck", q_heads, all_keys, preferred_element_type=jnp.float32) * factor
    )
    key_index = jnp.arange(old_len + fresh_rows, dtype=jnp.int32)[None, :]
    row_index = jnp.arange(fresh_rows, dtype=jnp.int32)[:, None]
    allowed = jnp.where(key_index < old_len, key_index < start_at, key_index - old_len <= row_index)
    scores = jnp.where(allowed[None], scores, NEG)
    row_peak = jnp.max(scores, axis=-1, keepdims=True)
    expd = jnp.exp(scores - row_peak)
    weights = (expd / jnp.sum(expd, axis=-1, keepdims=True)).astype(jnp.bfloat16)
    return jnp.einsum(
        "gck,kd->cgd", weights, all_values, preferred_element_type=jnp.float32
    ).astype(jnp.bfloat16)


def decode_attend(q_heads, key_old, value_old, key_self, value_self, lengths):
    factor = q_heads.shape[-1] ** (-0.5)
    past = jnp.einsum("bgd,bld->bgl", q_heads, key_old, preferred_element_type=jnp.float32) * factor
    slot_index = jnp.arange(key_old.shape[1], dtype=jnp.int32)
    past = jnp.where(slot_index[None, None, :] < lengths[:, None, None], past, NEG)
    own_score = (
        jnp.einsum("bgd,bd->bg", q_heads, key_self, preferred_element_type=jnp.float32) * factor
    )
    row_peak = jnp.maximum(jnp.max(past, axis=-1), own_score)
    past_exp = jnp.exp(past - row_peak[..., None])
    own_exp = jnp.exp(own_score - row_peak)
    row_total = jnp.sum(past_exp, axis=-1) + own_exp
    past_w = (past_exp / row_total[..., None]).astype(jnp.bfloat16)
    own_w = (own_exp / row_total).astype(jnp.bfloat16)
    summed = jnp.einsum("bgl,bld->bgd", past_w, value_old, preferred_element_type=jnp.float32)
    summed = (
        summed + own_w.astype(jnp.float32)[..., None] * value_self.astype(jnp.float32)[:, None, :]
    )
    return summed.astype(jnp.bfloat16)


def regroup(rows_in):
    return lax.all_to_all(rows_in, ("req", "kv"), split_axis=0, concat_axis=0, tiled=True)


def shards(
    hidden_in,
    slot_tokens,
    cache_len,
    prefill_start,
    key_cache,
    value_cache,
    key_prefix,
    value_prefix,
    attn_gain,
    q_proj,
    k_proj,
    v_proj,
    q_gain,
    k_gain,
    o_proj,
    ffn_gain,
    w_gate,
    w_up,
    w_down,
    final_gain,
    lm_head,
):
    req_count = lax.axis_size("req")
    kv_count = lax.axis_size("kv")
    devices = req_count * kv_count
    rows_dev = hidden_in.shape[0]
    kv_index = lax.axis_index("kv")
    self_index = lax.axis_index("req") * kv_count + kv_index
    slot_table = slot_tokens.reshape(devices, rows_dev)
    from_self = slot_table // rows_dev == self_index
    send_rows = jnp.sum(jnp.where(from_self, slot_table - self_index * rows_dev, 0), axis=1)
    slot_place = lax.dynamic_index_in_dim(slot_table, self_index, 0, keepdims=False) // rows_dev
    arrived = regroup(hidden_in[send_rows])
    owner_rows = arrived[slot_place]
    rows_all = lax.all_gather(owner_rows, "kv", axis=0, tiled=True)
    normed = norm_rows(rows_all, attn_gain).astype(jnp.bfloat16)
    o_full = lax.all_gather(o_proj, "kv", axis=0, tiled=True)
    ff_dev = w_gate.shape[1]
    ff_piece = ff_dev // kv_count
    gate_w = lax.all_gather(
        lax.dynamic_slice_in_dim(w_gate, kv_index * ff_piece, ff_piece, axis=1),
        "req",
        axis=1,
        tiled=True,
    )
    up_w = lax.all_gather(
        lax.dynamic_slice_in_dim(w_up, kv_index * ff_piece, ff_piece, axis=1),
        "req",
        axis=1,
        tiled=True,
    )
    down_w = lax.all_gather(
        lax.dynamic_slice_in_dim(w_down, kv_index * ff_piece, ff_piece, axis=0),
        "req",
        axis=0,
        tiled=True,
    )
    q_cols = q_proj.shape[1]
    kv_cols = k_proj.shape[1]
    projected = jnp.concatenate(
        [
            jnp.dot(normed, q_proj, preferred_element_type=jnp.float32),
            jnp.dot(normed, k_proj, preferred_element_type=jnp.float32),
            jnp.dot(normed, v_proj, preferred_element_type=jnp.float32),
        ],
        axis=1,
    )
    tok_req = projected.shape[0]
    head_dim = q_gain.shape[0]
    dec_count = cache_len.shape[0]
    fresh_count = tok_req - dec_count
    q_raw = projected[:, :q_cols].reshape(tok_req, q_cols // head_dim, head_dim)
    k_raw = projected[:, q_cols : q_cols + kv_cols].reshape(tok_req, kv_cols // head_dim, head_dim)
    v_new = (
        projected[:, q_cols + kv_cols :]
        .astype(jnp.bfloat16)
        .reshape(tok_req, kv_cols // head_dim, head_dim)
    )
    places = jnp.concatenate(
        [prefill_start[0] + jnp.arange(fresh_count, dtype=jnp.int32), cache_len]
    ).astype(jnp.float32)
    queries = rotate(norm_rows(q_raw, q_gain), places).astype(jnp.bfloat16)
    keys_new = rotate(norm_rows(k_raw, k_gain), places).astype(jnp.bfloat16)
    pre_out = prefill_full(
        queries[:fresh_count],
        key_prefix[0, :, 0:head_dim],
        value_prefix[0, :, 0:head_dim],
        keys_new[:fresh_count, 0],
        v_new[:fresh_count, 0],
        prefill_start[0],
    )
    dec_out = decode_attend(
        queries[fresh_count:],
        key_cache,
        value_cache,
        keys_new[fresh_count:, 0],
        v_new[fresh_count:, 0],
        cache_len,
    )
    pieces = jnp.concatenate([pre_out, dec_out], axis=0)
    pieces, gate_w, up_w, down_w = lax.optimization_barrier((pieces, gate_w, up_w, down_w))
    attended = lax.all_gather(pieces.reshape(tok_req, q_cols), "kv", axis=1, tiled=True)
    resid = (
        rows_all.astype(jnp.float32) + jnp.dot(attended, o_full, preferred_element_type=jnp.float32)
    ).astype(jnp.bfloat16)
    ffn_in = norm_rows(resid, ffn_gain).astype(jnp.bfloat16)
    gate_part = jnp.dot(ffn_in, gate_w, preferred_element_type=jnp.float32)
    up_part = jnp.dot(ffn_in, up_w, preferred_element_type=jnp.float32)
    hidden_act = (jax.nn.silu(gate_part) * up_part).astype(jnp.bfloat16)
    down_part = jnp.dot(hidden_act, down_w, preferred_element_type=jnp.float32)
    ffn_part = lax.psum_scatter(down_part, "kv", scatter_dimension=0, tiled=True)
    mine = lax.dynamic_slice_in_dim(resid, kv_index * rows_dev, rows_dev, axis=0)
    out_rows = (mine.astype(jnp.float32) + ffn_part).astype(jnp.bfloat16)
    going_back = jnp.zeros_like(out_rows).at[slot_place].set(out_rows)
    returned = regroup(going_back)
    layer_out = jnp.zeros_like(hidden_in).at[send_rows].set(returned)
    tail_sum = lax.psum(down_part[fresh_count - 1 :], "kv")
    tail_out = (resid[fresh_count - 1 :].astype(jnp.float32) + tail_sum).astype(jnp.bfloat16)
    tail_rows = norm_rows(tail_out, final_gain).astype(jnp.bfloat16)
    local_peaks = jnp.max(
        jnp.dot(
            lax.all_gather(tail_rows, "req", axis=0, tiled=True),
            lm_head,
            preferred_element_type=jnp.float32,
        ),
        axis=1,
    )
    max_logit = lax.pmax(local_peaks, ("req", "kv"))
    return (layer_out, max_logit)


def solution(mesh):
    placed = (
        P(("req", "kv"), None),
        P(),
        P("req"),
        P("req"),
        P("req", None, "kv"),
        P("req", None, "kv"),
        P("req", None, "kv"),
        P("req", None, "kv"),
        P(),
        P(None, "kv"),
        P(None, "kv"),
        P(None, "kv"),
        P(),
        P(),
        P("kv", None),
        P(),
        P(None, "req"),
        P(None, "req"),
        P("req", None),
        P(),
        P(None, ("req", "kv")),
    )
    return jax.shard_map(
        shards, mesh=mesh, in_specs=placed, out_specs=(P(("req", "kv"), None), P()), check_vma=False
    )
```

profile of v0, /device:TPU:1, one launch (start us, length us, event | category | flops | bytes accessed | tf_op | source)
XLA Modules:
  0.0 573.7 jit_solution(5138658079195809557)
XLA Ops:
  8.3 2.6 gather_fusion
  13.5 11.5 %all-to-all-start = ((bf16[128,2,1024]{2,1,0:T(2,128)(2,1)}), bf16[128,2,1024]{2,1,0:T(2,128)(2,1)S(1)}, u32[]{:S(2)}, u32[]{:S(2)}) async-start(bf16[128,2,1024]{2,1,0:T(2,128)(2,1)} %reshape.450), calls=%async_computation | async-start | bytes 1048576 | tf_op jit(solution)/shard_map/all_to_all | solution.py:77
  25.8 13.0 %all-to-all-done = bf16[128,2,1024]{2,1,0:T(2,128)(2,1)S(1)} async-done(((bf16[128,2,1024]{2,1,0:T(2,128)(2,1)}), bf16[128,2,1024]{2,1,0:T(2,128)(2,1)S(1)}, u32[]{:S(2)}, u32[]{:S(2)}) %all-to-all-start) | async-done | bytes 524320 | tf_op jit(solution)/shard_map/all_to_all | solution.py:77
  50.5 4.0 fusion.4
  54.5 15.7 %all-gather.19.cloned.1.call-done = bf16[1024,2048]{1,0:T(8,128)(2,1)} async-done(((bf16[128,2048]{1,0:T(8,128)(2,1)}), bf16[1024,2048]{1,0:T(8,128)(2,1)}) %all-gather.19.cloned.1.call-update) | async-done | bytes 4194320 | tf_op jit(solution)/shard_map/all_gather | solution.py:115
  70.1 3.2 fusion.10
  78.7 3.7 multiply_reduce_fusion.1
  88.2 3.6 convolution_convert_fusion
  92.6 15.9 %fusion.78 = (f32[2,1016]{1,0:T(2,128)S(1)}, f32[2,1016,3064]{2,1,0:T(8,128)}) fusion(pred[1016,3064]{1,0:T(8,128)(4,1)} %fusion.4, bf16[1016,128]{1,0:T(8,128)(2,1)S(1)} %copy.47, bf16[2048,128]{1,0:T(8,128)(2,1)S(1)} %bitcast.93, bf16[1024,2,64]{2,0,1:T(8,128)(2,1)S(1)} %get-tuple-element.10, bf16[1024,2,64]{2,0,1:T(8,128)(2,1)S(1)} %get-tuple-element.11), kind=kOutput, calls=%fused_computation.144 | convolution fusion | flops 1621384704 | bytes 29334016 | tf_op jit(solution)/shard_map/sub | solution.py:48
  108.5 12.0 %fusion.18 = bf16[1016,2,128]{2,0,1:T(8,128)(2,1)S(1)} fusion(f32[2,1016,3064]{2,1,0:T(8,128)} %get-tuple-element.25, f32[2,1016]{1,0:T(2,128)S(1)} %get-tuple-element.24, bf16[1016,128]{1,0:T(8,128)(2,1)S(1)} %slice.54, bf16[2048,128]{1,0:T(8,128)(2,1)S(1)} %bitcast.94), kind=kOutput, calls=%fused_computation.32 | convolution fusion | flops 1608149248 | bytes 26216896 | tf_op jit(solution)/shard_map/gck,kd->cgd/dot_general | solution.py:50
  120.6 48.2 %all-gather.11.cloned.1.call-done = bf16[2048,768]{0,1:T(8,128)(2,1)} async-done(((bf16[2048,48]{0,1:T(8,128)(2,1)}), bf16[2048,768]{0,1:T(8,128)(2,1)}) %all-gather.11.cloned.1.call-update) | async-done | bytes 3145744 | tf_op jit(solution)/shard_map/all_gather | solution.py:126
  168.8 48.9 %all-gather.13.cloned.1.call-done = bf16[768,2048]{1,0:T(8,128)(2,1)} async-done(((bf16[48,2048]{1,0:T(8,128)(2,1)}), bf16[768,2048]{1,0:T(8,128)(2,1)}) %all-gather.13.cloned.1.call-update) | async-done | bytes 3145744 | tf_op jit(solution)/shard_map/all_gather | solution.py:132
  218.8 49.7 %all-gather.17.cloned.1.call-done = bf16[2048,2048]{1,0:T(8,128)(2,1)} async-done(((bf16[256,2048]{1,0:T(8,128)(2,1)}), bf16[2048,2048]{1,0:T(8,128)(2,1)}) %all-gather.17.cloned.1.call-update) | async-done | bytes 8388624 | tf_op jit(solution)/shard_map/all_gather | solution.py:117
  268.5 34.4 %all-gather.15.cloned.1.call-done = bf16[1024,2048]{0,1:T(8,128)(2,1)} async-done(((bf16[1024,256]{0,1:T(8,128)(2,1)}), bf16[1024,2048]{0,1:T(8,128)(2,1)}) %all-gather.15.cloned.1.call-update) | async-done | bytes 4194320 | tf_op jit(solution)/shard_map/all_gather | solution.py:182
  302.9 14.2 %fusion.7 = (f32[1024]{0:T(1024)S(1)}, bf16[1024,2048]{1,0:T(8,128)(2,1)S(1)}) fusion(bf16[1024,2048]{0,1:T(8,128)(2,1)} %all-gather.15.cloned.1.call-done, bf16[2048,2048]{1,0:T(8,128)(2,1)} %all-gather.17.cloned.1.call-done, bf16[1024,2048]{1,0:T(8,128)(2,1)} %all-gather.19.cloned.1.call-done), kind=kOutput, calls=%fused_computation.20 | convolution fusion | flops 8602516480 | bytes 20975616 | tf_op jit(solution)/shard_map/dot_general | solution.py:184
  319.0 7.1 %fusion.20 = f32[1024,768]{1,0:T(8,128)} fusion(bf16[2048,768]{0,1:T(8,128)(2,1)} %all-gather.9.cloned.1.call-done, bf16[1024,2048]{1,0:T(8,128)(2,1)S(1)} %get-tuple-element.27, f32[2048]{0:T(1024)S(1)} %copy-done.17, f32[1024]{0:T(1024)S(1)} %add_rsqrt_fusion.1), kind=kOutput, calls=%fused_computation.33 | convolution fusion | flops 3229614080 | bytes 10498048 | tf_op jit(solution)/shard_map/dot_general | solution.py:187
  326.2 14.1 %fusion.23 = f32[1024,2048]{1,0:T(8,128)} fusion(bf16[768,2048]{1,0:T(8,128)(2,1)} %all-gather.13.cloned.1.call-done, f32[1024,768]{1,0:T(8,128)} %fusion.20, bf16[2048,768]{0,1:T(8,128)(2,1)} %all-gather.11.cloned.1.call-done, bf16[1024,2048]{1,0:T(8,128)(2,1)} %copy-done.7, f32[2048]{0:T(1024)S(1)} %copy-done.17, f32[1024]{0:T(1024)S(1)} %add_rsqrt_fusion.1), kind=kOutput, calls=%fused_computation.34 | convolution fusion | flops 6455558144 | bytes 22032384 | tf_op jit(solution)/shard_map/dot_general | solution.py:190
  342.6 56.0 %all-reduce.2.cloned.1.call-done = f32[9,2048]{1,0:T(8,128)} async-done(((f32[9,2048]{1,0:T(8,128)}), f32[9,2048]{1,0:T(8,128)}) %all-reduce.2.cloned.1.call-update) | async-done | bytes 73744 | tf_op jit(solution)/shard_map/psum | solution.py:197
  400.6 53.5 %reduce-scatter.2.cloned.1.call-done = f32[128,2048]{1,0:T(8,128)} async-done(((f32[1024,2048]{1,0:T(8,128)}), f32[128,2048]{1,0:T(8,128)}) %reduce-scatter.2.cloned.1.call-update) | async-done | bytes 1048592 | tf_op jit(solution)/shard_map/reduce_scatter | solution.py:191
  454.1 2.6 scatter_custom_fusion
  458.9 8.4 %all-to-all-start.1 = ((bf16[128,2,1024]{2,1,0:T(2,128)(2,1)}), bf16[128,2,1024]{2,1,0:T(2,128)(2,1)S(1)}, u32[]{:S(2)}, u32[]{:S(2)}) async-start(bf16[128,2,1024]{2,1,0:T(2,128)(2,1)} %reshape.452), calls=%async_computation.2 | async-start | bytes 1048576 | tf_op jit(solution)/shard_map/all_to_all | solution.py:77
  467.3 22.4 %all-gather.1 = bf16[16,9,2048]{2,1,0:T(8,128)(2,1)S(1)} all-gather(bf16[1,9,2048]{2,1,0:T(8,128)(2,1)S(1)} %fusion.51), channel_id=1, replica_groups=mesh['req'=16,'kv'=8] {'req'}, dimensions={0}, use_global_device_ids=true | all-gather | bytes 626688 | tf_op jit(solution)/shard_map/all_gather | solution.py:202
  490.8 4.4 convolution_reduce_fusion
  495.2 68.5 %pmax.7 = f32[144]{0:T(256)} all-reduce(f32[144]{0:T(256)S(1)} %convolution_reduce_fusion), channel_id=1, replica_groups=mesh['req'=16,'kv'=8] {'req','kv'}, use_global_device_ids=true, to_apply=%region_15.16 | all-reduce | flops 144 | bytes 1152 | tf_op jit(solution)/shard_map/pmax | solution.py:208
  (114 shorter events, 40.7 us)
Async XLA Ops:
  7.2 34.2 %copy-start = (bf16[2048,384]{1,0:T(8,128)(2,1)S(1)}, bf16[2048,384]{1,0:T(8,128)(2,1)}, u32[]{:S(2)}) copy-start(bf16[2048,384]{1,0:T(8,128)(2,1)} %param.37) | copy-start | bytes 4718596
  13.5 25.2 %all-to-all-start = ((bf16[128,2,1024]{2,1,0:T(2,128)(2,1)}), bf16[128,2,1024]{2,1,0:T(2,128)(2,1)S(1)}, u32[]{:S(2)}, u32[]{:S(2)}) async-start(bf16[128,2,1024]{2,1,0:T(2,128)(2,1)} %reshape.450), calls=%async_computation | async-start | bytes 1048576 | tf_op jit(solution)/shard_map/all_to_all | solution.py:77
  25.0 45.1 %all-gather.19.cloned.1.call-start = ((), (), s32[]{:S(2)}) async-start(), calls=%async_computation.10 | async-start | bytes 4718592 | tf_op jit(solution)/shard_map/all_gather | solution.py:115
  41.2 7.1 %copy-start.10 = (s32[8]{0:T(128)S(1)}, s32[8]{0:T(128)}, u32[]{:S(2)}) copy-start(s32[8]{0:T(128)} %param.23) | copy-start | bytes 100
  41.3 79.3 %all-gather.9.cloned.1.call-start = ((), (), s32[]{:S(2)}) async-start(), calls=%async_computation.3 | async-start | bytes 3342336 | tf_op jit(solution)/shard_map/all_gather | solution.py:120
  42.5 126.3 %all-gather.11.cloned.1.call-start = ((), (), s32[]{:S(2)}) async-start(), calls=%async_computation.4 | async-start | bytes 3342336 | tf_op jit(solution)/shard_map/all_gather | solution.py:126
  44.8 172.8 %all-gather.13.cloned.1.call-start = ((), (), s32[]{:S(2)}) async-start(), calls=%async_computation.5 | async-start | bytes 3342336 | tf_op jit(solution)/shard_map/all_gather | solution.py:132
  46.5 221.9 %all-gather.17.cloned.1.call-start = ((), (), s32[]{:S(2)}) async-start(), calls=%async_computation.7 | async-start | bytes 9437184 | tf_op jit(solution)/shard_map/all_gather | solution.py:117
  47.1 255.8 %all-gather.15.cloned.1.call-start = ((), (), s32[]{:S(2)}) async-start(), calls=%async_computation.6 | async-start | bytes 4718592 | tf_op jit(solution)/shard_map/all_gather | solution.py:182
  48.5 24.9 %copy-start.8 = (f32[2048]{0:T(1024)S(1)}, f32[2048]{0:T(1024)}, u32[]{:S(2)}) copy-start(f32[2048]{0:T(1024)} %param.29) | copy-start | bytes 24580
  70.1 3.4 copy-start.2
  74.8 3.9 copy-start.6
  77.1 5.3 copy-start.11
  78.7 5.4 copy-start.12
  84.9 3.2 copy-start.14
  88.1 3.7 copy-start.5
  88.2 4.5 copy-start.15
  92.6 15.9 %copy-start.16 = (bf16[1,2048,128]{2,1,0:T(8,128)(2,1)S(1)}, bf16[1,2048,128]{2,1,0:T(8,128)(2,1)}, u32[]{:S(2)}) copy-start(bf16[1,2048,128]{2,1,0:T(8,128)(2,1)} %param.28) | copy-start | bytes 1572868
  218.7 100.3 %copy-start.17 = (f32[2048]{0:T(1024)S(1)}, f32[2048]{0:T(1024)}, u32[]{:S(2)}) copy-start(f32[2048]{0:T(1024)} %param.36) | copy-start | bytes 24580
  218.7 179.8 %all-reduce.2.cloned.1.call-start = ((), (), s32[]{:S(2)}) async-start(), calls=%async_computation.9 | async-start | bytes 262144 | tf_op jit(solution)/shard_map/psum | solution.py:197
  341.8 57.8 %copy-start.9 = (f32[2048]{0:T(1024)S(1)}, f32[2048]{0:T(1024)}, u32[]{:S(2)}) copy-start(f32[2048]{0:T(1024)} %param.40) | copy-start | bytes 24580
  341.8 112.3 %reduce-scatter.2.cloned.1.call-start = ((), (), s32[]{:S(2)}) async-start(), calls=%async_computation.8 | async-start | bytes 9437184 | tf_op jit(solution)/shard_map/reduce_scatter | solution.py:191
  458.9 104.8 %all-to-all-start.1 = ((bf16[128,2,1024]{2,1,0:T(2,128)(2,1)}), bf16[128,2,1024]{2,1,0:T(2,128)(2,1)S(1)}, u32[]{:S(2)}, u32[]{:S(2)}) async-start(bf16[128,2,1024]{2,1,0:T(2,128)(2,1)} %reshape.452), calls=%async_computation.2 | async-start | bytes 1048576 | tf_op jit(solution)/shard_map/all_to_all | solution.py:77
  489.7 76.9 %copy-start.1 = (bf16[2048,384]{1,0:T(8,128)(2,1)S(1)}, bf16[2048,384]{1,0:T(8,128)(2,1)}, u32[]{:S(2)}) copy-start(bf16[2048,384]{1,0:T(8,128)(2,1)} %param.37) | copy-start | bytes 4718596
  (4 other events, 7.7 us)
Sparse Core Ops, SparseCore 0:
  41.4 28.7 all-gather.18
  72.3 47.3 all-gather.8
  121.8 46.8 all-gather.10
  170.8 46.8 all-gather.12
  219.2 49.1 all-gather.16
  270.6 32.2 all-gather.14
  341.9 56.5 all-reduce.1
  401.1 52.9 reduce-scatter.1
where the time goes:
time: 578 us; the launch traced here: 574 us
  waiting for transfers between devices  321 us (56%)
  blocking collectives  90.9 us (16%)
  matrix products  79.3 us (14%)
  local copies, waits for them, and re-layouts  24.9 us (4%)
  other arithmetic  21.6 us (4%)
  starting transfers between devices  20.8 us (4%)
  between operations  15.5 us (3%)
    pmax x1, blocking collectives, shards(): max_logit = lax.pmax(local_peaks, ('req', 'kv'))  68.5 us
    psum x1, waiting for transfers between devices, shards(): tail_sum = lax.psum(down_part[fresh_count - 1:], 'kv')  56 us
    reduce_scatter x1, waiting for transfers between devices, shards(): lax.psum_scatter(down_part, 'kv', scatter_dimension=0, tiled=True)  53.5 us
    all_gather x1, waiting for transfers between devices, shards(): o_full = lax.all_gather(o_proj, 'kv', axis=0, tiled=True)  49.7 us
    all_gather x1, waiting for transfers between devices, shards(): lax.all_gather(lax.dynamic_slice_in_dim(w_down, kv_index * ff_piece, ff_p...  48.9 us
    all_gather x1, waiting for transfers between devices, shards(): lax.all_gather(lax.dynamic_slice_in_dim(w_up, kv_index * ff_piece, ff_pie...  48.2 us
    all_gather x1, waiting for transfers between devices, shards(): lax.all_gather(pieces.reshape(tok_req, q_cols), 'kv', axis=1, tiled=True)  34.4 us
    all_gather x1, blocking collectives, shards(): lax.all_gather(tail_rows, 'req', axis=0, tiled=True)  22.4 us
  transfers between devices with their start and end apart: 10, of which 8 were waited for; matrix products, arithmetic and copies ran while one was open for 12% of the time, Pallas kernels for 0%

commit v1 on v0

--- a/solution.py
+++ b/solution.py
@@ -194,7 +194,7 @@
     going_back = jnp.zeros_like(out_rows).at[slot_place].set(out_rows)
     returned = regroup(going_back)
     layer_out = jnp.zeros_like(hidden_in).at[send_rows].set(returned)
-    tail_sum = lax.psum(down_part[fresh_count - 1 :], "kv")
+    tail_sum = jnp.sum(lax.all_gather(down_part[fresh_count - 1 :], "kv"), axis=0)
     tail_out = (resid[fresh_count - 1 :].astype(jnp.float32) + tail_sum).astype(jnp.bfloat16)
     tail_rows = norm_rows(tail_out, final_gain).astype(jnp.bfloat16)
     local_peaks = jnp.max(

time: 578 us -> 516 us (0.89)
  waiting for transfers between devices: 321 us -> 245 us
  blocking collectives: 90.9 us -> 105 us
    psum x1 -> x0, waiting for transfers between devices: 56 us -> none  [shards(): tail_sum = lax.psum(down_part[fresh_count - 1:], 'kv')]
    reduce_scatter x1, waiting for transfers between devices: 53.5 us -> 35 us  [shards(): lax.psum_scatter(down_part, 'kv', scatter_dimension=0, tiled=True)]
    all_gather x0 -> x1, blocking collectives: none -> 14.4 us  [shards(): lax.all_gather(down_part[fresh_count - 1:], 'kv')]
  transfers between devices with their start and end apart: 10 -> 9, of which waited for: 8 -> 7; matrix products, arithmetic and copies ran while one was open for 12% -> 14% of each run, Pallas kernels for 0% -> 0%
where the time goes in v1:
time: 516 us; the launch traced here: 512 us
  waiting for transfers between devices  245 us (47%)
  blocking collectives  105 us (20%)
  matrix products  79.3 us (15%)
  local copies, waits for them, and re-layouts  24.2 us (5%)
  other arithmetic  21.6 us (4%)
  starting transfers between devices  20.7 us (4%)
  between operations  15.5 us (3%)
    pmax x1, blocking collectives, shards(): max_logit = lax.pmax(local_peaks, ('req', 'kv'))  68.4 us
    all_gather x1, waiting for transfers between devices, shards(): o_full = lax.all_gather(o_proj, 'kv', axis=0, tiled=True)  49.7 us
    all_gather x1, waiting for transfers between devices, shards(): lax.all_gather(lax.dynamic_slice_in_dim(w_down, kv_index * ff_piece, ff_p...  48.9 us
    all_gather x1, waiting for transfers between devices, shards(): lax.all_gather(lax.dynamic_slice_in_dim(w_up, kv_index * ff_piece, ff_pie...  48.2 us
    reduce_scatter x1, waiting for transfers between devices, shards(): lax.psum_scatter(down_part, 'kv', scatter_dimension=0, tiled=True)  35 us
    all_gather x1, waiting for transfers between devices, shards(): lax.all_gather(pieces.reshape(tok_req, q_cols), 'kv', axis=1, tiled=True)  34.4 us
    all_gather x1, blocking collectives, shards(): lax.all_gather(tail_rows, 'req', axis=0, tiled=True)  22.4 us
    all_to_all x2, starting transfers between devices, regroup(): lax.all_to_all(rows_in, ('req', 'kv'), split_axis=0, concat_axis=0, tiled...  19.9 us
  transfers between devices with their start and end apart: 9, of which 7 were waited for; matrix products, arithmetic and copies ran while one was open for 14% of the time, Pallas kernels for 0%

profile of v1, /device:TPU:1, one launch (start us, length us, event | category | flops | bytes accessed | tf_op | source)
XLA Modules:
  0.0 511.9 jit_solution(16865209602947537836)
XLA Ops:
  8.3 2.6 gather_fusion
  13.5 11.5 %all-to-all-start = ((bf16[128,2,1024]{2,1,0:T(2,128)(2,1)}), bf16[128,2,1024]{2,1,0:T(2,128)(2,1)S(1)}, u32[]{:S(2)}, u32[]{:S(2)}) async-start(bf16[128,2,1024]{2,1,0:T(2,128)(2,1)} %reshape.454), calls=%async_computation | async-start | bytes 1048576 | tf_op jit(solution)/shard_map/all_to_all | solution.py:77
  25.8 13.0 %all-to-all-done = bf16[128,2,1024]{2,1,0:T(2,128)(2,1)S(1)} async-done(((bf16[128,2,1024]{2,1,0:T(2,128)(2,1)}), bf16[128,2,1024]{2,1,0:T(2,128)(2,1)S(1)}, u32[]{:S(2)}, u32[]{:S(2)}) %all-to-all-start) | async-done | bytes 524320 | tf_op jit(solution)/shard_map/all_to_all | solution.py:77
  50.5 4.0 fusion.4
  54.5 15.6 %all-gather.21.cloned.1.call-done = bf16[1024,2048]{1,0:T(8,128)(2,1)} async-done(((bf16[128,2048]{1,0:T(8,128)(2,1)}), bf16[1024,2048]{1,0:T(8,128)(2,1)}) %all-gather.21.cloned.1.call-update) | async-done | bytes 4194320 | tf_op jit(solution)/shard_map/all_gather | solution.py:115
  70.1 3.2 fusion.10
  78.7 3.7 multiply_reduce_fusion.1
  88.2 3.6 convolution_convert_fusion
  92.6 15.9 %fusion.78 = (f32[2,1016]{1,0:T(2,128)S(1)}, f32[2,1016,3064]{2,1,0:T(8,128)}) fusion(pred[1016,3064]{1,0:T(8,128)(4,1)} %fusion.4, bf16[1016,128]{1,0:T(8,128)(2,1)S(1)} %copy.47, bf16[2048,128]{1,0:T(8,128)(2,1)S(1)} %bitcast.95, bf16[1024,2,64]{2,0,1:T(8,128)(2,1)S(1)} %get-tuple-element.10, bf16[1024,2,64]{2,0,1:T(8,128)(2,1)S(1)} %get-tuple-element.11), kind=kOutput, calls=%fused_computation.145 | convolution fusion | flops 1621384704 | bytes 29334016 | tf_op jit(solution)/shard_map/sub | solution.py:48
  108.5 12.0 %fusion.18 = bf16[1016,2,128]{2,0,1:T(8,128)(2,1)S(1)} fusion(f32[2,1016,3064]{2,1,0:T(8,128)} %get-tuple-element.25, f32[2,1016]{1,0:T(2,128)S(1)} %get-tuple-element.24, bf16[1016,128]{1,0:T(8,128)(2,1)S(1)} %slice.54, bf16[2048,128]{1,0:T(8,128)(2,1)S(1)} %bitcast.96), kind=kOutput, calls=%fused_computation.32 | convolution fusion | flops 1608149248 | bytes 26216896 | tf_op jit(solution)/shard_map/gck,kd->cgd/dot_general | solution.py:50
  120.5 48.2 %all-gather.13.cloned.1.call-done = bf16[2048,768]{0,1:T(8,128)(2,1)} async-done(((bf16[2048,48]{0,1:T(8,128)(2,1)}), bf16[2048,768]{0,1:T(8,128)(2,1)}) %all-gather.13.cloned.1.call-update) | async-done | bytes 3145744 | tf_op jit(solution)/shard_map/all_gather | solution.py:126
  168.8 48.9 %all-gather.15.cloned.1.call-done = bf16[768,2048]{1,0:T(8,128)(2,1)} async-done(((bf16[48,2048]{1,0:T(8,128)(2,1)}), bf16[768,2048]{1,0:T(8,128)(2,1)}) %all-gather.15.cloned.1.call-update) | async-done | bytes 3145744 | tf_op jit(solution)/shard_map/all_gather | solution.py:132
  218.8 49.7 %all-gather.19.cloned.1.call-done = bf16[2048,2048]{1,0:T(8,128)(2,1)} async-done(((bf16[256,2048]{1,0:T(8,128)(2,1)}), bf16[2048,2048]{1,0:T(8,128)(2,1)}) %all-gather.19.cloned.1.call-update) | async-done | bytes 8388624 | tf_op jit(solution)/shard_map/all_gather | solution.py:117
  268.5 34.4 %all-gather.17.cloned.1.call-done = bf16[1024,2048]{0,1:T(8,128)(2,1)} async-done(((bf16[1024,256]{0,1:T(8,128)(2,1)}), bf16[1024,2048]{0,1:T(8,128)(2,1)}) %all-gather.17.cloned.1.call-update) | async-done | bytes 4194320 | tf_op jit(solution)/shard_map/all_gather | solution.py:182
  302.9 14.2 %fusion.7 = (f32[1024]{0:T(1024)S(1)}, bf16[1024,2048]{1,0:T(8,128)(2,1)S(1)}) fusion(bf16[1024,2048]{0,1:T(8,128)(2,1)} %all-gather.17.cloned.1.call-done, bf16[2048,2048]{1,0:T(8,128)(2,1)} %all-gather.19.cloned.1.call-done, bf16[1024,2048]{1,0:T(8,128)(2,1)} %all-gather.21.cloned.1.call-done), kind=kOutput, calls=%fused_computation.20 | convolution fusion | flops 8602516480 | bytes 20975616 | tf_op jit(solution)/shard_map/dot_general | solution.py:184
  319.0 7.1 %fusion.20 = f32[1024,768]{1,0:T(8,128)} fusion(bf16[2048,768]{0,1:T(8,128)(2,1)} %all-gather.11.cloned.1.call-done, bf16[1024,2048]{1,0:T(8,128)(2,1)S(1)} %get-tuple-element.27, f32[2048]{0:T(1024)S(1)} %copy-done.17, f32[1024]{0:T(1024)S(1)} %add_rsqrt_fusion.1), kind=kOutput, calls=%fused_computation.33 | convolution fusion | flops 3229614080 | bytes 10498048 | tf_op jit(solution)/shard_map/dot_general | solution.py:187
  326.2 14.1 %fusion.23 = f32[1024,2048]{1,0:T(8,128)} fusion(bf16[768,2048]{1,0:T(8,128)(2,1)} %all-gather.15.cloned.1.call-done, f32[1024,768]{1,0:T(8,128)} %fusion.20, bf16[2048,768]{0,1:T(8,128)(2,1)} %all-gather.13.cloned.1.call-done, bf16[1024,2048]{1,0:T(8,128)(2,1)} %copy-done.7, f32[2048]{0:T(1024)S(1)} %copy-done.17, f32[1024]{0:T(1024)S(1)} %add_rsqrt_fusion.1), kind=kOutput, calls=%fused_computation.34 | convolution fusion | flops 6455558144 | bytes 22032384 | tf_op jit(solution)/shard_map/dot_general | solution.py:190
  341.2 14.4 %all-gather.2 = f32[8,9,2048]{2,1,0:T(8,128)S(1)} all-gather(f32[1,9,2048]{2,1,0:T(8,128)S(1)} %slice_bitcast_fusion), channel_id=3, replica_groups=mesh['req'=16,'kv'=8] {'kv'}, dimensions={0}, use_global_device_ids=true | all-gather | bytes 663552 | tf_op jit(solution)/shard_map/all_gather | solution.py:197
  357.6 35.0 %reduce-scatter.2.cloned.1.call-done = f32[128,2048]{1,0:T(8,128)} async-done(((f32[1024,2048]{1,0:T(8,128)}), f32[128,2048]{1,0:T(8,128)}) %reduce-scatter.2.cloned.1.call-update) | async-done | bytes 1048592 | tf_op jit(solution)/shard_map/reduce_scatter | solution.py:191
  392.5 2.6 scatter_custom_fusion
  397.3 8.4 %all-to-all-start.1 = ((bf16[128,2,1024]{2,1,0:T(2,128)(2,1)}), bf16[128,2,1024]{2,1,0:T(2,128)(2,1)S(1)}, u32[]{:S(2)}, u32[]{:S(2)}) async-start(bf16[128,2,1024]{2,1,0:T(2,128)(2,1)} %reshape.456), calls=%async_computation.2 | async-start | bytes 1048576 | tf_op jit(solution)/shard_map/all_to_all | solution.py:77
  405.7 22.4 %all-gather.3 = bf16[16,9,2048]{2,1,0:T(8,128)(2,1)S(1)} all-gather(bf16[1,9,2048]{2,1,0:T(8,128)(2,1)S(1)} %fusion.51), channel_id=1, replica_groups=mesh['req'=16,'kv'=8] {'req'}, dimensions={0}, use_global_device_ids=true | all-gather | bytes 626688 | tf_op jit(solution)/shard_map/all_gather | solution.py:202
  429.2 4.4 convolution_reduce_fusion
  433.6 68.4 %pmax.7 = f32[144]{0:T(256)} all-reduce(f32[144]{0:T(256)S(1)} %convolution_reduce_fusion), channel_id=1, replica_groups=mesh['req'=16,'kv'=8] {'req','kv'}, use_global_device_ids=true, to_apply=%region_15.16 | all-reduce | flops 144 | bytes 1152 | tf_op jit(solution)/shard_map/pmax | solution.py:208
  (113 shorter events, 39.3 us)
Async XLA Ops:
  7.2 34.2 %copy-start = (bf16[2048,384]{1,0:T(8,128)(2,1)S(1)}, bf16[2048,384]{1,0:T(8,128)(2,1)}, u32[]{:S(2)}) copy-start(bf16[2048,384]{1,0:T(8,128)(2,1)} %param.37) | copy-start | bytes 4718596
  13.5 25.2 %all-to-all-start = ((bf16[128,2,1024]{2,1,0:T(2,128)(2,1)}), bf16[128,2,1024]{2,1,0:T(2,128)(2,1)S(1)}, u32[]{:S(2)}, u32[]{:S(2)}) async-start(bf16[128,2,1024]{2,1,0:T(2,128)(2,1)} %reshape.454), calls=%async_computation | async-start | bytes 1048576 | tf_op jit(solution)/shard_map/all_to_all | solution.py:77
  25.0 45.1 %all-gather.21.cloned.1.call-start = ((), (), s32[]{:S(2)}) async-start(), calls=%async_computation.9 | async-start | bytes 4718592 | tf_op jit(solution)/shard_map/all_gather | solution.py:115
  41.2 7.2 %copy-start.10 = (s32[8]{0:T(128)S(1)}, s32[8]{0:T(128)}, u32[]{:S(2)}) copy-start(s32[8]{0:T(128)} %param.23) | copy-start | bytes 100
  41.3 79.3 %all-gather.11.cloned.1.call-start = ((), (), s32[]{:S(2)}) async-start(), calls=%async_computation.3 | async-start | bytes 3342336 | tf_op jit(solution)/shard_map/all_gather | solution.py:120
  42.5 126.3 %all-gather.13.cloned.1.call-start = ((), (), s32[]{:S(2)}) async-start(), calls=%async_computation.4 | async-start | bytes 3342336 | tf_op jit(solution)/shard_map/all_gather | solution.py:126
  44.9 172.8 %all-gather.15.cloned.1.call-start = ((), (), s32[]{:S(2)}) async-start(), calls=%async_computation.5 | async-start | bytes 3342336 | tf_op jit(solution)/shard_map/all_gather | solution.py:132
  46.6 221.9 %all-gather.19.cloned.1.call-start = ((), (), s32[]{:S(2)}) async-start(), calls=%async_computation.7 | async-start | bytes 9437184 | tf_op jit(solution)/shard_map/all_gather | solution.py:117
  47.2 255.7 %all-gather.17.cloned.1.call-start = ((), (), s32[]{:S(2)}) async-start(), calls=%async_computation.6 | async-start | bytes 4718592 | tf_op jit(solution)/shard_map/all_gather | solution.py:182
  48.5 24.9 %copy-start.8 = (f32[2048]{0:T(1024)S(1)}, f32[2048]{0:T(1024)}, u32[]{:S(2)}) copy-start(f32[2048]{0:T(1024)} %param.29) | copy-start | bytes 24580
  70.1 3.4 copy-start.2
  74.8 2.3 copy-start.3
  74.8 3.9 copy-start.6
  77.1 5.3 %copy-start.11 = (f32[128]{0:T(128)S(1)}, f32[128]{0:T(128)}, u32[]{:S(2)}) copy-start(f32[128]{0:T(128)} %param.34) | copy-start | bytes 1540
  78.7 5.4 %copy-start.12 = (f32[128]{0:T(128)S(1)}, f32[128]{0:T(128)}, u32[]{:S(2)}) copy-start(f32[128]{0:T(128)} %param.33) | copy-start | bytes 1540
  84.9 3.2 copy-start.14
  88.1 3.7 copy-start.5
  88.2 4.5 copy-start.15
  92.6 15.9 %copy-start.16 = (bf16[1,2048,128]{2,1,0:T(8,128)(2,1)S(1)}, bf16[1,2048,128]{2,1,0:T(8,128)(2,1)}, u32[]{:S(2)}) copy-start(bf16[1,2048,128]{2,1,0:T(8,128)(2,1)} %param.28) | copy-start | bytes 1572868
  218.7 100.3 %copy-start.17 = (f32[2048]{0:T(1024)S(1)}, f32[2048]{0:T(1024)}, u32[]{:S(2)}) copy-start(f32[2048]{0:T(1024)} %param.36) | copy-start | bytes 24580
  218.7 173.8 %reduce-scatter.2.cloned.1.call-start = ((), (), s32[]{:S(2)}) async-start(), calls=%async_computation.8 | async-start | bytes 9437184 | tf_op jit(solution)/shard_map/reduce_scatter | solution.py:191
  340.2 16.4 %copy-start.9 = (f32[2048]{0:T(1024)S(1)}, f32[2048]{0:T(1024)}, u32[]{:S(2)}) copy-start(f32[2048]{0:T(1024)} %param.40) | copy-start | bytes 24580
  397.3 104.7 %all-to-all-start.1 = ((bf16[128,2,1024]{2,1,0:T(2,128)(2,1)}), bf16[128,2,1024]{2,1,0:T(2,128)(2,1)S(1)}, u32[]{:S(2)}, u32[]{:S(2)}) async-start(bf16[128,2,1024]{2,1,0:T(2,128)(2,1)} %reshape.456), calls=%async_computation.2 | async-start | bytes 1048576 | tf_op jit(solution)/shard_map/all_to_all | solution.py:77
  428.1 76.7 %copy-start.1 = (bf16[2048,384]{1,0:T(8,128)(2,1)S(1)}, bf16[2048,384]{1,0:T(8,128)(2,1)}, u32[]{:S(2)}) copy-start(bf16[2048,384]{1,0:T(8,128)(2,1)} %param.37) | copy-start | bytes 4718596
  (3 other events, 5.4 us)
Sparse Core Ops, SparseCore 0:
  41.4 28.7 all-gather.20
  72.3 47.3 all-gather.10
  121.8 46.8 all-gather.12
  170.7 46.8 all-gather.14
  219.2 49.1 all-gather.18
  270.6 32.2 all-gather.16
  340.4 52.1 reduce-scatter.1
